TPU v7x, 512 devices: a whole 4x8x8 slice. The times are simulated.
512 devices in a mesh: ctx: 32 (over y, x), head: 16 (over z, core).
Axes of the slice: x: 4, y: 8, z: 8, core: 2. Of those that a mesh axis runs over, the one named last changes fastest.
Arguments:
- activations: bfloat16 [8192, 16384], P('ctx'), may hold values from -6 to 6
- w_query: bfloat16 [16384, 2048], P('ctx', 'head'), may hold values from -0.046875 to 0.046875
- w_keyval: bfloat16 [16384, 256], P('ctx', 'head'), may hold values from -0.046875 to 0.046875
- f_query: bfloat16 [16, 128, 128], P('head'), may hold values from -1 to 1
- f_key: bfloat16 [128, 128], replicated, may hold values from -1 to 1
- w_out: bfloat16 [2048, 16384], P('ctx', 'head'), may hold values from -0.75 to 0.75
Outputs:
- sublayer_out: bfloat16 [8192, 16384], P('ctx', 'head')
All inputs are finite; a program needn't handle non-finite values.
Results may differ from a plain program's by a relative error of at most 0.0086.
Values may be sent and summed in bfloat16 or wider, within the bound.
A program may use at most 64 MiB of HBM per device.

v0:
```python
import math
import jax
import jax.numpy as jnp
from jax import lax
from jax.sharding import PartitionSpec as P

WINDOW = 64


def from_behind(array, axis, by):
    size = lax.axis_size(axis)
    pairs = [(i, i + by) for i in range(size) if 0 <= i + by < size]
    return lax.ppermute(array, axis, pairs)


def prefix(array, axis, combine, identity):
    size, mine = (lax.axis_size(axis), lax.axis_index(axis))
    everything = jax.tree.map(
        lambda part, kind: lax.all_gather(part.astype(kind), axis),
        array,
        jax.tree.map(lambda a: jnp.bfloat16 if a.dtype == jnp.float32 else a.dtype, array),
    )
    start = jax.tree.map(
        lambda part, zero: jnp.broadcast_to(jnp.asarray(zero, part.dtype), part.shape),
        array,
        identity,
    )

    def step(k, before):
        reached = k < mine
        new = combine(
            before, jax.tree.map(lambda part, own: part[k].astype(own.dtype), everything, array)
        )
        return jax.tree.map(lambda a, b: jnp.where(reached, a, b), new, before)

    return lax.fori_loop(0, size, step, start)


def normalized(logits):
    rising = jnp.exp(logits)
    falling = jnp.exp(-logits)
    rising = rising / jnp.sum(rising, axis=-1, keepdims=True)
    falling = falling / jnp.sum(falling, axis=-1, keepdims=True)
    return jnp.concatenate([rising, falling], axis=-1).astype(jnp.bfloat16)


def state_of(features, values):
    matrix = jnp.einsum("nf,nc->fc", features, values, preferred_element_type=jnp.float32)
    totals = jnp.sum(features.astype(jnp.float32), axis=0)
    return (matrix, totals)


def add_states(earlier, later):
    return (earlier[0] + later[0], earlier[1] + later[1])


def per_device(activations, w_query, w_keyval, f_query, f_key, w_out):
    length = activations.shape[0]
    head_width = f_key.shape[0]
    local_heads = f_query.shape[0]
    columns = activations
    query_sum = jnp.dot(
        columns,
        lax.all_gather(w_query, "ctx", axis=0, tiled=True),
        preferred_element_type=jnp.float32,
    )
    pair_sum = jnp.dot(
        columns,
        lax.all_gather(w_keyval, "ctx", axis=0, tiled=True),
        preferred_element_type=jnp.float32,
    )
    queries = query_sum.astype(jnp.bfloat16)
    keyval = lax.all_gather(pair_sum.astype(jnp.bfloat16), "head", axis=1, tiled=True)
    border = from_behind(keyval[length - WINDOW :], "ctx", 1)
    extended = jnp.concatenate([border, keyval], axis=0)
    ext_keys = extended[:, :head_width]
    ext_vals = extended[:, head_width:]
    first_pos = lax.axis_index("ctx") * length - WINDOW
    present = first_pos + jnp.arange(length + WINDOW) >= 0
    ext_feats = normalized(jnp.dot(ext_keys, f_key, preferred_element_type=jnp.float32))
    ext_feats = jnp.where(present[:, None], ext_feats, jnp.zeros_like(ext_feats))
    contribution = state_of(ext_feats[:length], ext_vals[:length])
    identity = (
        jnp.zeros((2 * head_width, head_width), jnp.float32),
        jnp.zeros((2 * head_width,), jnp.float32),
    )
    matrix, totals = prefix(contribution, "ctx", add_states, identity)
    query_heads = queries.reshape(length, local_heads, head_width)
    query_feats = normalized(
        jnp.einsum("thc,hcf->htf", query_heads, f_query, preferred_element_type=jnp.float32)
    )
    offsets = jnp.arange(length)[:, None] + WINDOW - jnp.arange(length + WINDOW)[None, :]
    inside = (offsets >= 0) & (offsets < WINDOW) & present[None, :]
    beyond = (offsets >= WINDOW) & present[None, :]
    scale = 1.0 / math.sqrt(head_width)
    scores = (
        jnp.einsum("thc,kc->htk", query_heads, ext_keys, preferred_element_type=jnp.float32) * scale
    )
    near_w = jnp.where(inside[None], jnp.exp(scores), 0.0)
    far_w = jnp.where(
        beyond[None],
        jnp.einsum("htf,kf->htk", query_feats, ext_feats, preferred_element_type=jnp.float32),
        0.0,
    )
    weights = near_w + far_w
    feats_wide = query_feats.astype(jnp.float32)
    numerator = jnp.einsum(
        "htk,kc->htc", weights, ext_vals.astype(jnp.float32), precision=lax.Precision.HIGHEST
    )
    numerator = numerator + jnp.einsum(
        "htf,fc->htc", feats_wide, matrix, precision=lax.Precision.HIGHEST
    )
    denominator = jnp.sum(weights, axis=-1) + jnp.einsum(
        "htf,f->ht", feats_wide, totals, precision=lax.Precision.HIGHEST
    )
    attn_heads = (numerator / denominator[..., None]).astype(jnp.bfloat16)
    attn_rows = jnp.transpose(attn_heads, (1, 0, 2)).reshape(length, local_heads * head_width)
    all_heads = lax.all_gather(attn_rows, "head", axis=1, tiled=True)
    columns = all_heads
    projected = jnp.dot(
        columns,
        lax.all_gather(w_out, "ctx", axis=0, tiled=True),
        preferred_element_type=jnp.float32,
    )
    return projected.astype(jnp.bfloat16)


def solution(mesh):
    in_specs = (
        P("ctx", None),
        P("ctx", "head"),
        P("ctx", "head"),
        P("head", None, None),
        P(),
        P("ctx", "head"),
    )
    out_specs = P("ctx", "head")
    return jax.shard_map(
        per_device, mesh=mesh, in_specs=in_specs, out_specs=out_specs, check_vma=False
    )
```

profile of v0, /device:TPU:1, one launch (start us, length us, event | category | flops | bytes accessed | tf_op | source)
XLA Modules:
  0.0 402.4 jit_solution(3140013990136511824)
XLA Ops:
  6.5 39.9 %all_gather.27 = bf16[16384,16]{0,1:T(8,128)(2,1)S(1)} all-gather(bf16[512,16]{0,1:T(8,128)(2,1)} %param.10), channel_id=1, replica_groups=mesh['ctx'=32,'head'=16] {'ctx'}, dimensions={0}, use_global_device_ids=true | all-gather | bytes 540672 | tf_op jit(solution)/shard_map/all_gather | solution.py:69
  46.5 5.6 %convolution_convert_fusion.3 = bf16[256,16]{0,1:T(8,128)(2,1)S(1)} fusion(bf16[256,16384]{1,0:T(8,128)(2,1)} %param.8, bf16[16384,16]{0,1:T(8,128)(2,1)S(1)} %all_gather.27), kind=kOutput, calls=%fused_computation.16 | convolution fusion | flops 134221824 | bytes 8921088 | tf_op jit(solution)/shard_map/dot_general | solution.py:67
  52.1 35.5 %all_gather.28 = bf16[256,256]{0,1:T(8,128)(2,1)S(1)} all-gather(bf16[256,16]{0,1:T(8,128)(2,1)S(1)} %convolution_convert_fusion.3), channel_id=1, replica_groups=mesh['ctx'=32,'head'=16] {'head'}, dimensions={1}, use_global_device_ids=true | all-gather | bytes 139264 | tf_op jit(solution)/shard_map/all_gather | solution.py:73
  87.6 0.1 slice.21
  87.7 2.4 collective-permute-start
  90.1 1.3 collective-permute-done
  91.4 0.5 exponential_reduce_fusion
  91.9 0.2 divide_convert_fusion.1
  92.1 0.1 maximum_select_fusion
  92.2 0.9 convolution_convert_fusion.1
  93.1 0.0 all-gather.14.cloned.1.call-update
  93.1 0.0 all-gather.8.cloned.1.call-start
  93.2 0.7 all-gather.8.cloned.1.call-update
  93.9 0.0 all-gather.12.cloned.1.call-start
  93.9 0.7 all-gather.12.cloned.1.call-update
  94.6 0.0 all-gather.10.cloned.1.call-start
  94.7 0.1 slice_reduce_fusion
  94.7 35.3 %all-gather.2 = bf16[32,1,256]{2,1,0:T(2,128)(2,1)S(1)} all-gather(bf16[1,1,256]{2,1,0:T(2,128)(2,1)S(1)} %reshape.161), channel_id=3, replica_groups=mesh['ctx'=32,'head'=16] {'ctx'}, dimensions={0}, use_global_device_ids=true | all-gather | bytes 16896 | tf_op jit(solution)/shard_map/all_gather | solution.py:19
  130.0 41.1 %all-gather.14.cloned.1.call-done = bf16[8192,128]{1,0:T(8,128)(2,1)} async-done(((bf16[256,128]{1,0:T(8,128)(2,1)}), bf16[8192,128]{1,0:T(8,128)(2,1)}) %all-gather.14.cloned.1.call-update) | async-done | bytes 2097168 | tf_op jit(solution)/shard_map/all_gather | solution.py:19
  171.1 30.8 %while.16 = (s32[]{:T(128)}, f32[256,128]{1,0:T(8,128)S(1)}, f32[256]{0:T(256)S(1)}, s32[]{:T(128)}, bf16[32,256,128]{2,1,0:T(8,128)(2,1)}, /*index=5*/bf16[32,256]{1,0:T(8,128)(2,1)S(1)}, s32[]{:T(128)}, s32[]{:T(128)}) while((s32[]{:T(128)}, f32[256,128]{1,0:T(8,128)S(1)}, f32[256]{0:T(256)S(1)}, s32[]{:T(128)}, ...), condition=%wide.region_6.7_spmd.clone, body=%wide.region_5.6_spmd.clone.sunk | while | flops 132100 | bytes 332403 | solution.py:36
  171.1 0.9 add_select_fusion.4
  172.1 0.9 add_select_fusion.4
  173.1 0.9 add_select_fusion.4
  174.0 0.9 add_select_fusion.4
  175.0 0.9 add_select_fusion.4
  175.9 0.9 add_select_fusion.4
  176.9 0.9 add_select_fusion.4
  177.9 0.9 add_select_fusion.4
  178.8 0.9 add_select_fusion.4
  179.8 0.9 add_select_fusion.4
  180.8 0.9 add_select_fusion.4
  181.7 0.9 add_select_fusion.4
  182.7 0.9 add_select_fusion.4
  183.7 0.9 add_select_fusion.4
  184.6 0.9 add_select_fusion.4
  185.6 0.9 add_select_fusion.4
  186.6 0.9 add_select_fusion.4
  187.5 0.9 add_select_fusion.4
  188.5 0.9 add_select_fusion.4
  189.4 0.9 add_select_fusion.4
  190.4 0.9 add_select_fusion.4
  191.4 0.9 add_select_fusion.4
  192.3 0.9 add_select_fusion.4
  193.3 0.9 add_select_fusion.4
  194.3 0.9 add_select_fusion.4
  195.2 0.9 add_select_fusion.4
  196.2 0.9 add_select_fusion.4
  197.2 0.9 add_select_fusion.4
  198.1 0.9 add_select_fusion.4
  199.1 0.9 add_select_fusion.4
  200.1 0.9 add_select_fusion.4
  201.0 0.9 add_select_fusion.4
  202.0 58.0 %all-gather.8.cloned.1.call-done = bf16[16384,128]{1,0:T(8,128)(2,1)} async-done(((bf16[512,128]{1,0:T(8,128)(2,1)}), bf16[16384,128]{1,0:T(8,128)(2,1)}) %all-gather.8.cloned.1.call-update) | async-done | bytes 4194320 | tf_op jit(solution)/shard_map/all_gather | solution.py:64
  260.0 6.9 %convolution_convert_fusion.2 = bf16[256,128]{1,0:T(8,128)(2,1)S(1)} fusion(bf16[256,16384]{1,0:T(8,128)(2,1)} %param.8, bf16[16384,128]{1,0:T(8,128)(2,1)} %all-gather.8.cloned.1.call-done), kind=kOutput, calls=%fused_computation.15 | convolution fusion | flops 1073774592 | bytes 12648448 | tf_op jit(solution)/shard_map/dot_general | solution.py:62
  266.9 0.2 exponential_reduce_fusion.1
  267.2 0.2 fusion
  267.4 0.1 fusion.20
  267.6 0.4 fusion.32
  268.0 0.3 fusion.21
  268.3 1.2 fusion.6
  269.5 0.0 all-gather.10.cloned.1.call-update
  269.5 78.3 %all-gather.12.cloned.1.call-done = bf16[2048,1024]{1,0:T(8,128)(2,1)} async-done(((bf16[64,1024]{1,0:T(8,128)(2,1)}), bf16[2048,1024]{1,0:T(8,128)(2,1)}) %all-gather.12.cloned.1.call-update) | async-done | bytes 4194320 | tf_op jit(solution)/shard_map/all_gather | solution.py:122
  347.8 43.5 %all-gather.10.cloned.1.call-done = bf16[256,2048]{1,0:T(8,128)(2,1)} async-done(((bf16[256,128]{1,0:T(8,128)(2,1)}), bf16[256,2048]{1,0:T(8,128)(2,1)}) %all-gather.10.cloned.1.call-update) | async-done | bytes 1048592 | tf_op jit(solution)/shard_map/all_gather | solution.py:118
  391.3 4.6 %convolution_convert_fusion = bf16[256,1024]{1,0:T(8,128)(2,1)} fusion(bf16[256,2048]{1,0:T(8,128)(2,1)} %all-gather.10.cloned.1.call-done, bf16[2048,1024]{1,0:T(8,128)(2,1)} %all-gather.12.cloned.1.call-done), kind=kOutput, calls=%fused_computation.3 | convolution fusion | flops 1074003968 | bytes 5767168 | tf_op jit(solution)/shard_map/dot_general | solution.py:120
  (77 shorter events, 0.9 us)
Async XLA Ops:
  6.5 84.9 %copy-start = (bf16[128,128]{1,0:T(8,128)(2,1)S(1)}, bf16[128,128]{1,0:T(8,128)(2,1)}, u32[]{:S(2)}) copy-start(bf16[128,128]{1,0:T(8,128)(2,1)} %param.12) | copy-start | bytes 98308
  6.5 164.6 %all-gather.14.cloned.1.call-start = ((), (), s32[]{:S(2)}) async-start(), calls=%async_computation.3 | async-start | bytes 2162688 | tf_op jit(solution)/shard_map/all_gather | solution.py:19
  87.7 3.7 collective-permute-start
  93.1 166.9 %all-gather.8.cloned.1.call-start = ((), (), s32[]{:S(2)}) async-start(), calls=%async_computation | async-start | bytes 4325376 | tf_op jit(solution)/shard_map/all_gather | solution.py:64
  93.9 253.9 %all-gather.12.cloned.1.call-start = ((), (), s32[]{:S(2)}) async-start(), calls=%async_computation.2 | async-start | bytes 4325376 | tf_op jit(solution)/shard_map/all_gather | solution.py:122
  94.6 296.7 %all-gather.10.cloned.1.call-start = ((), (), s32[]{:S(2)}) async-start(), calls=%async_computation.1 | async-start | bytes 1114112 | tf_op jit(solution)/shard_map/all_gather | solution.py:118
  202.0 64.9 %copy-start.1 = (bf16[1,128,128]{2,1,0:T(8,128)(2,1)S(1)}, bf16[1,128,128]{2,1,0:T(8,128)(2,1)}, u32[]{:S(2)}) copy-start(bf16[1,128,128]{2,1,0:T(8,128)(2,1)} %param.11) | copy-start | bytes 98308
Sparse Core Ops, SparseCore 0:
  93.2 77.8 all-gather.13
  174.3 85.6 all-gather.7
  263.1 84.6 all-gather.11
  349.7 41.5 all-gather.9
where the time goes:
time: 404 us; the launch traced here: 402 us
  waiting for transfers between devices  224 us (55%)
  blocking collectives  111 us (27%)
  other arithmetic  30.2 us (7%)
  matrix products  21 us (5%)
  between operations  13.3 us (3%)
    all_gather x1, waiting for transfers between devices, per_device(): lax.all_gather(w_out, 'ctx', axis=0, tiled=True)  78.3 us
    all_gather x1, waiting for transfers between devices, per_device(): lax.all_gather(w_query, 'ctx', axis=0, tiled=True)  58 us
    all_gather x1, waiting for transfers between devices, per_device(): all_heads = lax.all_gather(attn_rows, 'head', axis=1, tiled=True)  43.5 us
    all_gather x1, waiting for transfers between devices, prefix(): lax.all_gather(part.astype(kind), axis)  41.1 us
    all_gather x1, blocking collectives, per_device(): lax.all_gather(w_keyval, 'ctx', axis=0, tiled=True)  39.9 us
    all_gather x1, blocking collectives, per_device(): lax.all_gather(pair_sum.astype(jnp.bfloat16), 'head', axis=1, tiled=True)  35.5 us
    all_gather x1, blocking collectives, prefix(): lax.all_gather(part.astype(kind), axis)  35.3 us
    select_n x64, other arithmetic, step(): return jax.tree.map(lambda a, b: jnp.where(reached, a, b), new, before)  29.3 us
  transfers between devices with their start and end apart: 5, of which 5 were waited for; matrix products, arithmetic and copies ran while one was open for 10% of the time, Pallas kernels for 0%

commit v1 on v0

--- a/solution.py
+++ b/solution.py
@@ -115,7 +115,12 @@
     )
     attn_heads = (numerator / denominator[..., None]).astype(jnp.bfloat16)
     attn_rows = jnp.transpose(attn_heads, (1, 0, 2)).reshape(length, local_heads * head_width)
-    all_heads = lax.all_gather(attn_rows, "head", axis=1, tiled=True)
+    ring = [attn_rows]
+    for hop in range(15):
+        ring.append(lax.ppermute(ring[-1], "head", [(dev, (dev + 1) % 16) for dev in range(16)]))
+    all_heads = jnp.roll(
+        jnp.concatenate(ring[::-1], axis=1), (lax.axis_index("head") + 1) * ring[0].shape[1], axis=1
+    )
     columns = all_heads
     projected = jnp.dot(
         columns,

time: 404 us -> 362 us (0.90)
  waiting for transfers between devices: 224 us -> 169 us
  starting transfers between devices: 2.53 us -> 14 us
    all_gather x1, waiting for transfers between devices: 78.3 us -> 6.15 us  [per_device(): lax.all_gather(w_out, 'ctx', axis=0, tiled=True)]
    ppermute x0 -> x15, waiting for transfers between devices: none -> 61 us  [per_device(): lax.ppermute(ring[-1], 'head', [(dev, (dev + 1) % 16) for dev in range(16)])]
    all_gather x1 -> x0, waiting for transfers between devices: 43.5 us -> none  [per_device(): all_heads = lax.all_gather(attn_rows, 'head', axis=1, tiled=True)]
    ppermute x0 -> x15, starting transfers between devices: none -> 11.5 us  [per_device(): lax.ppermute(ring[-1], 'head', [(dev, (dev + 1) % 16) for dev in range(16)])]
  transfers between devices with their start and end apart: 5 -> 19, of which waited for: 5 -> 19; matrix products, arithmetic and copies ran while one was open for 10% -> 11% of each run, Pallas kernels for 0% -> 0%
where the time goes in v1:
time: 362 us; the launch traced here: 359 us
  waiting for transfers between devices  169 us (47%)
  blocking collectives  110 us (30%)
  other arithmetic  30.1 us (8%)
  matrix products  19.8 us (5%)
  starting transfers between devices  14 us (4%)
  between operations  13.5 us (4%)
    ppermute x15, waiting for transfers between devices, per_device(): lax.ppermute(ring[-1], 'head', [(dev, (dev + 1) % 16) for dev in range(16)])  61 us
    all_gather x1, waiting for transfers between devices, per_device(): lax.all_gather(w_query, 'ctx', axis=0, tiled=True)  58 us
    all_gather x1, waiting for transfers between devices, prefix(): lax.all_gather(part.astype(kind), axis)  41.5 us
    all_gather x1, blocking collectives, per_device(): lax.all_gather(w_keyval, 'ctx', axis=0, tiled=True)  39.9 us
    all_gather x1, blocking collectives, per_device(): lax.all_gather(pair_sum.astype(jnp.bfloat16), 'head', axis=1, tiled=True)  35.5 us
    all_gather x1, blocking collectives, prefix(): lax.all_gather(part.astype(kind), axis)  35 us
    select_n x64, other arithmetic, step(): return jax.tree.map(lambda a, b: jnp.where(reached, a, b), new, before)  29.3 us
    ppermute x15, starting transfers between devices, per_device(): lax.ppermute(ring[-1], 'head', [(dev, (dev + 1) % 16) for dev in range(16)])  11.5 us
  transfers between devices with their start and end apart: 19, of which 19 were waited for; matrix products, arithmetic and copies ran while one was open for 11% of the time, Pallas kernels for 0%

profile of v1, /device:TPU:1, one launch (start us, length us, event | category | flops | bytes accessed | tf_op | source)
XLA Modules:
  0.0 358.6 jit_solution(9898811956056561982)
XLA Ops:
  6.5 39.9 %all_gather.24 = bf16[16384,16]{0,1:T(8,128)(2,1)S(1)} all-gather(bf16[512,16]{0,1:T(8,128)(2,1)} %param.10), channel_id=1, replica_groups=mesh['ctx'=32,'head'=16] {'ctx'}, dimensions={0}, use_global_device_ids=true | all-gather | bytes 540672 | tf_op jit(solution)/shard_map/all_gather | solution.py:69
  46.5 5.6 %convolution_convert_fusion.3 = bf16[256,16]{0,1:T(8,128)(2,1)S(1)} fusion(bf16[256,16384]{1,0:T(8,128)(2,1)} %param.8, bf16[16384,16]{0,1:T(8,128)(2,1)S(1)} %all_gather.24), kind=kOutput, calls=%fused_computation.16 | convolution fusion | flops 134221824 | bytes 8921088 | tf_op jit(solution)/shard_map/dot_general | solution.py:67
  52.1 35.5 %all_gather.25 = bf16[256,256]{0,1:T(8,128)(2,1)S(1)} all-gather(bf16[256,16]{0,1:T(8,128)(2,1)S(1)} %convolution_convert_fusion.3), channel_id=1, replica_groups=mesh['ctx'=32,'head'=16] {'head'}, dimensions={1}, use_global_device_ids=true | all-gather | bytes 139264 | tf_op jit(solution)/shard_map/all_gather | solution.py:73
  87.7 2.4 collective-permute-start
  90.1 1.3 collective-permute-done
  92.2 0.9 convolution_convert_fusion.1
  94.7 35.0 %all-gather.2 = bf16[32,1,256]{2,1,0:T(2,128)(2,1)S(1)} all-gather(bf16[1,1,256]{2,1,0:T(2,128)(2,1)S(1)} %reshape.161), channel_id=3, replica_groups=mesh['ctx'=32,'head'=16] {'ctx'}, dimensions={0}, use_global_device_ids=true | all-gather | bytes 16896 | tf_op jit(solution)/shard_map/all_gather | solution.py:19
  129.7 41.5 %all-gather.11.cloned.1.call-done = bf16[8192,128]{1,0:T(8,128)(2,1)} async-done(((bf16[256,128]{1,0:T(8,128)(2,1)}), bf16[8192,128]{1,0:T(8,128)(2,1)}) %all-gather.11.cloned.1.call-update) | async-done | bytes 2097168 | tf_op jit(solution)/shard_map/all_gather | solution.py:19
  171.1 30.8 %while.16 = (s32[]{:T(128)}, f32[256,128]{1,0:T(8,128)S(1)}, f32[256]{0:T(256)S(1)}, s32[]{:T(128)}, bf16[32,256,128]{2,1,0:T(8,128)(2,1)}, /*index=5*/bf16[32,256]{1,0:T(8,128)(2,1)S(1)}, s32[]{:T(128)}, s32[]{:T(128)}) while((s32[]{:T(128)}, f32[256,128]{1,0:T(8,128)S(1)}, f32[256]{0:T(256)S(1)}, s32[]{:T(128)}, ...), condition=%wide.region_6.7_spmd.clone, body=%wide.region_5.6_spmd.clone.sunk | while | flops 132100 | bytes 332403 | solution.py:36
  171.1 0.9 add_select_fusion.4
  172.1 0.9 add_select_fusion.4
  173.1 0.9 add_select_fusion.4
  174.0 0.9 add_select_fusion.4
  175.0 0.9 add_select_fusion.4
  175.9 0.9 add_select_fusion.4
  176.9 0.9 add_select_fusion.4
  177.9 0.9 add_select_fusion.4
  178.8 0.9 add_select_fusion.4
  179.8 0.9 add_select_fusion.4
  180.8 0.9 add_select_fusion.4
  181.7 0.9 add_select_fusion.4
  182.7 0.9 add_select_fusion.4
  183.6 0.9 add_select_fusion.4
  184.6 0.9 add_select_fusion.4
  185.6 0.9 add_select_fusion.4
  186.5 0.9 add_select_fusion.4
  187.5 0.9 add_select_fusion.4
  188.5 0.9 add_select_fusion.4
  189.4 0.9 add_select_fusion.4
  190.4 0.9 add_select_fusion.4
  191.4 0.9 add_select_fusion.4
  192.3 0.9 add_select_fusion.4
  193.3 0.9 add_select_fusion.4
  194.2 0.9 add_select_fusion.4
  195.2 0.9 add_select_fusion.4
  196.2 0.9 add_select_fusion.4
  197.1 0.9 add_select_fusion.4
  198.1 0.9 add_select_fusion.4
  199.1 0.9 add_select_fusion.4
  200.0 0.9 add_select_fusion.4
  201.0 0.9 add_select_fusion.4
  201.9 58.0 %all-gather.7.cloned.1.call-done = bf16[16384,128]{1,0:T(8,128)(2,1)} async-done(((bf16[512,128]{1,0:T(8,128)(2,1)}), bf16[16384,128]{1,0:T(8,128)(2,1)}) %all-gather.7.cloned.1.call-update) | async-done | bytes 4194320 | tf_op jit(solution)/shard_map/all_gather | solution.py:64
  260.0 6.9 %convolution_convert_fusion.2 = bf16[256,128]{1,0:T(8,128)(2,1)S(1)} fusion(bf16[256,16384]{1,0:T(8,128)(2,1)} %param.8, bf16[16384,128]{1,0:T(8,128)(2,1)} %all-gather.7.cloned.1.call-done), kind=kOutput, calls=%fused_computation.15 | convolution fusion | flops 1073774592 | bytes 12648448 | tf_op jit(solution)/shard_map/dot_general | solution.py:62
  268.6 4.4 %collective-permute-start.1 = (bf16[256,128]{0,1:T(8,128)(2,1)S(1)}, bf16[256,128]{0,1:T(8,128)(2,1)S(1)}, u32[]{:S(2)}, u32[]{:S(2)}) collective-permute-start(bf16[256,128]{0,1:T(8,128)(2,1)S(1)} %fusion.6), channel_id=1, source_target_pairs={{0,1},{1,2},{2,3},{3,4},{4,5},{5,6},{6,7},{7,8},{8,9},{9,10},{10,1... | collective-permute-start | bytes 196616 | tf_op jit(solution)/shard_map/ppermute | solution.py:120
  273.1 1.3 collective-permute-done.1
  274.4 2.4 collective-permute-start.2
  276.7 1.3 collective-permute-done.2
  278.1 2.4 collective-permute-start.3
  280.4 1.9 collective-permute-done.3
  282.4 1.8 collective-permute-start.4
  284.1 3.1 collective-permute-done.4
  287.8 4.3 %collective-permute-done.5 = bf16[256,128]{0,1:T(8,128)(2,1)S(1)} collective-permute-done((bf16[256,128]{0,1:T(8,128)(2,1)S(1)}, bf16[256,128]{0,1:T(8,128)(2,1)S(1)}, u32[]{:S(2)}, u32[]{:S(2)}) %collective-permute-start.5) | collective-permute-done | bytes 65568 | tf_op jit(solution)/shard_map/ppermute | solution.py:120
  292.2 4.9 %collective-permute-done.6 = bf16[256,128]{0,1:T(8,128)(2,1)S(1)} collective-permute-done((bf16[256,128]{0,1:T(8,128)(2,1)S(1)}, bf16[256,128]{0,1:T(8,128)(2,1)S(1)}, u32[]{:S(2)}, u32[]{:S(2)}) %collective-permute-start.6) | collective-permute-done | bytes 65568 | tf_op jit(solution)/shard_map/ppermute | solution.py:120
  297.1 4.9 %collective-permute-done.7 = bf16[256,128]{0,1:T(8,128)(2,1)S(1)} collective-permute-done((bf16[256,128]{0,1:T(8,128)(2,1)S(1)}, bf16[256,128]{0,1:T(8,128)(2,1)S(1)}, u32[]{:S(2)}, u32[]{:S(2)}) %collective-permute-start.7) | collective-permute-done | bytes 65568 | tf_op jit(solution)/shard_map/ppermute | solution.py:120
  302.0 4.9 %collective-permute-done.8 = bf16[256,128]{0,1:T(8,128)(2,1)S(1)} collective-permute-done((bf16[256,128]{0,1:T(8,128)(2,1)S(1)}, bf16[256,128]{0,1:T(8,128)(2,1)S(1)}, u32[]{:S(2)}, u32[]{:S(2)}) %collective-permute-start.8) | collective-permute-done | bytes 65568 | tf_op jit(solution)/shard_map/ppermute | solution.py:120
  306.9 4.9 %collective-permute-done.9 = bf16[256,128]{0,1:T(8,128)(2,1)S(1)} collective-permute-done((bf16[256,128]{0,1:T(8,128)(2,1)S(1)}, bf16[256,128]{0,1:T(8,128)(2,1)S(1)}, u32[]{:S(2)}, u32[]{:S(2)}) %collective-permute-start.9) | collective-permute-done | bytes 65568 | tf_op jit(solution)/shard_map/ppermute | solution.py:120
  311.8 4.9 %collective-permute-done.10 = bf16[256,128]{0,1:T(8,128)(2,1)S(1)} collective-permute-done((bf16[256,128]{0,1:T(8,128)(2,1)S(1)}, bf16[256,128]{0,1:T(8,128)(2,1)S(1)}, u32[]{:S(2)}, u32[]{:S(2)}) %collective-permute-start.10) | collective-permute-done | bytes 65568 | tf_op jit(solution)/shard_map/ppermute | solution.py:120
  316.7 4.9 %collective-permute-done.11 = bf16[256,128]{0,1:T(8,128)(2,1)S(1)} collective-permute-done((bf16[256,128]{0,1:T(8,128)(2,1)S(1)}, bf16[256,128]{0,1:T(8,128)(2,1)S(1)}, u32[]{:S(2)}, u32[]{:S(2)}) %collective-permute-start.11) | collective-permute-done | bytes 65568 | tf_op jit(solution)/shard_map/ppermute | solution.py:120
  321.6 4.9 %collective-permute-done.12 = bf16[256,128]{0,1:T(8,128)(2,1)S(1)} collective-permute-done((bf16[256,128]{0,1:T(8,128)(2,1)S(1)}, bf16[256,128]{0,1:T(8,128)(2,1)S(1)}, u32[]{:S(2)}, u32[]{:S(2)}) %collective-permute-start.12) | collective-permute-done | bytes 65568 | tf_op jit(solution)/shard_map/ppermute | solution.py:120
  326.5 4.9 %collective-permute-done.13 = bf16[256,128]{0,1:T(8,128)(2,1)S(1)} collective-permute-done((bf16[256,128]{0,1:T(8,128)(2,1)S(1)}, bf16[256,128]{0,1:T(8,128)(2,1)S(1)}, u32[]{:S(2)}, u32[]{:S(2)}) %collective-permute-start.13) | collective-permute-done | bytes 65568 | tf_op jit(solution)/shard_map/ppermute | solution.py:120
  331.4 4.9 %collective-permute-done.14 = bf16[256,128]{0,1:T(8,128)(2,1)S(1)} collective-permute-done((bf16[256,128]{0,1:T(8,128)(2,1)S(1)}, bf16[256,128]{0,1:T(8,128)(2,1)S(1)}, u32[]{:S(2)}, u32[]{:S(2)}) %collective-permute-start.14) | collective-permute-done | bytes 65568 | tf_op jit(solution)/shard_map/ppermute | solution.py:120
  336.3 4.9 %collective-permute-done.15 = bf16[256,128]{0,1:T(8,128)(2,1)S(1)} collective-permute-done((bf16[256,128]{0,1:T(8,128)(2,1)S(1)}, bf16[256,128]{0,1:T(8,128)(2,1)S(1)}, u32[]{:S(2)}, u32[]{:S(2)}) %collective-permute-start.15) | collective-permute-done | bytes 65568 | tf_op jit(solution)/shard_map/ppermute | solution.py:120
  341.6 6.2 %all-gather.9.cloned.1.call-done = bf16[2048,1024]{1,0:T(8,128)(2,1)} async-done(((bf16[64,1024]{1,0:T(8,128)(2,1)}), bf16[2048,1024]{1,0:T(8,128)(2,1)}) %all-gather.9.cloned.1.call-update) | async-done | bytes 4194320 | tf_op jit(solution)/shard_map/all_gather | solution.py:127
  347.8 4.3 %convolution_convert_fusion = bf16[256,1024]{1,0:T(8,128)(2,1)} fusion(bf16[2048,1024]{1,0:T(8,128)(2,1)} %all-gather.9.cloned.1.call-done, bf16[256,4096]{0,1:T(8,128)(2,1)S(1)} %constant_dynamic-update-slice_fusion, s32[]{:T(128)S(6)} %select_n.70), kind=kOutput, calls=%fused_computation.3 | convolution fusion | flops 1074003968 | bytes 5767172 | tf_op jit(solution)/shard_map/dot_general | solution.py:125
  (136 shorter events, 5.7 us)
Async XLA Ops:
  6.5 84.9 %copy-start = (bf16[128,128]{1,0:T(8,128)(2,1)S(1)}, bf16[128,128]{1,0:T(8,128)(2,1)}, u32[]{:S(2)}) copy-start(bf16[128,128]{1,0:T(8,128)(2,1)} %param.12) | copy-start | bytes 98308
  6.5 164.6 %all-gather.11.cloned.1.call-start = ((), (), s32[]{:S(2)}) async-start(), calls=%async_computation.2 | async-start | bytes 2162688 | tf_op jit(solution)/shard_map/all_gather | solution.py:19
  87.7 3.7 %collective-permute-start = (bf16[64,256]{0,1:T(8,128)(2,1)S(1)}, bf16[64,256]{0,1:T(8,128)(2,1)S(1)}, u32[]{:S(2)}, u32[]{:S(2)}) collective-permute-start(bf16[64,256]{0,1:T(8,128)(2,1)S(1)} %slice.21), channel_id=1, source_target_pairs={{0,16},{16,32},{32,48},{48,64},{64,80},{80,96},{96,112},{112,128},... | collective-permute-start | bytes 98312 | tf_op jit(solution)/shard_map/ppermute | solution.py:13
  93.1 166.9 %all-gather.7.cloned.1.call-start = ((), (), s32[]{:S(2)}) async-start(), calls=%async_computation | async-start | bytes 4325376 | tf_op jit(solution)/shard_map/all_gather | solution.py:64
  93.9 253.9 %all-gather.9.cloned.1.call-start = ((), (), s32[]{:S(2)}) async-start(), calls=%async_computation.1 | async-start | bytes 4325376 | tf_op jit(solution)/shard_map/all_gather | solution.py:127
  201.9 64.9 %copy-start.1 = (bf16[1,128,128]{2,1,0:T(8,128)(2,1)S(1)}, bf16[1,128,128]{2,1,0:T(8,128)(2,1)}, u32[]{:S(2)}) copy-start(bf16[1,128,128]{2,1,0:T(8,128)(2,1)} %param.11) | copy-start | bytes 98308
  268.6 5.8 %collective-permute-start.1 = (bf16[256,128]{0,1:T(8,128)(2,1)S(1)}, bf16[256,128]{0,1:T(8,128)(2,1)S(1)}, u32[]{:S(2)}, u32[]{:S(2)}) collective-permute-start(bf16[256,128]{0,1:T(8,128)(2,1)S(1)} %fusion.6), channel_id=1, source_target_pairs={{0,1},{1,2},{2,3},{3,4},{4,5},{5,6},{6,7},{7,8},{8,9},{9,10},{10,1... | collective-permute-start | bytes 196616 | tf_op jit(solution)/shard_map/ppermute | solution.py:120
  274.4 3.7 %collective-permute-start.2 = (bf16[256,128]{0,1:T(8,128)(2,1)S(1)}, bf16[256,128]{0,1:T(8,128)(2,1)S(1)}, u32[]{:S(2)}, u32[]{:S(2)}) collective-permute-start(bf16[256,128]{0,1:T(8,128)(2,1)S(1)} %collective-permute-done.1), channel_id=1, source_target_pairs={{0,1},{1,2},{2,3},{3,4},{4,5},{5,6},{6,7},{7,8},{8,9},{9,10},{10,1... | collective-permute-start | bytes 196616 | tf_op jit(solution)/shard_map/ppermute | solution.py:120
  278.1 4.3 %collective-permute-start.3 = (bf16[256,128]{0,1:T(8,128)(2,1)S(1)}, bf16[256,128]{0,1:T(8,128)(2,1)S(1)}, u32[]{:S(2)}, u32[]{:S(2)}) collective-permute-start(bf16[256,128]{0,1:T(8,128)(2,1)S(1)} %collective-permute-done.2), channel_id=1, source_target_pairs={{0,1},{1,2},{2,3},{3,4},{4,5},{5,6},{6,7},{7,8},{8,9},{9,10},{10,1... | collective-permute-start | bytes 196616 | tf_op jit(solution)/shard_map/ppermute | solution.py:120
  282.4 4.9 %collective-permute-start.4 = (bf16[256,128]{0,1:T(8,128)(2,1)S(1)}, bf16[256,128]{0,1:T(8,128)(2,1)S(1)}, u32[]{:S(2)}, u32[]{:S(2)}) collective-permute-start(bf16[256,128]{0,1:T(8,128)(2,1)S(1)} %collective-permute-done.3), channel_id=1, source_target_pairs={{0,1},{1,2},{2,3},{3,4},{4,5},{5,6},{6,7},{7,8},{8,9},{9,10},{10,1... | collective-permute-start | bytes 196616 | tf_op jit(solution)/shard_map/ppermute | solution.py:120
  287.3 4.9 %collective-permute-start.5 = (bf16[256,128]{0,1:T(8,128)(2,1)S(1)}, bf16[256,128]{0,1:T(8,128)(2,1)S(1)}, u32[]{:S(2)}, u32[]{:S(2)}) collective-permute-start(bf16[256,128]{0,1:T(8,128)(2,1)S(1)} %collective-permute-done.4), channel_id=1, source_target_pairs={{0,1},{1,2},{2,3},{3,4},{4,5},{5,6},{6,7},{7,8},{8,9},{9,10},{10,1... | collective-permute-start | bytes 196616 | tf_op jit(solution)/shard_map/ppermute | solution.py:120
  292.2 4.9 %collective-permute-start.6 = (bf16[256,128]{0,1:T(8,128)(2,1)S(1)}, bf16[256,128]{0,1:T(8,128)(2,1)S(1)}, u32[]{:S(2)}, u32[]{:S(2)}) collective-permute-start(bf16[256,128]{0,1:T(8,128)(2,1)S(1)} %collective-permute-done.5), channel_id=1, source_target_pairs={{0,1},{1,2},{2,3},{3,4},{4,5},{5,6},{6,7},{7,8},{8,9},{9,10},{10,1... | collective-permute-start | bytes 196616 | tf_op jit(solution)/shard_map/ppermute | solution.py:120
  297.1 4.9 %collective-permute-start.7 = (bf16[256,128]{0,1:T(8,128)(2,1)S(1)}, bf16[256,128]{0,1:T(8,128)(2,1)S(1)}, u32[]{:S(2)}, u32[]{:S(2)}) collective-permute-start(bf16[256,128]{0,1:T(8,128)(2,1)S(1)} %collective-permute-done.6), channel_id=1, source_target_pairs={{0,1},{1,2},{2,3},{3,4},{4,5},{5,6},{6,7},{7,8},{8,9},{9,10},{10,1... | collective-permute-start | bytes 196616 | tf_op jit(solution)/shard_map/ppermute | solution.py:120
  302.0 4.9 %collective-permute-start.8 = (bf16[256,128]{0,1:T(8,128)(2,1)S(1)}, bf16[256,128]{0,1:T(8,128)(2,1)S(1)}, u32[]{:S(2)}, u32[]{:S(2)}) collective-permute-start(bf16[256,128]{0,1:T(8,128)(2,1)S(1)} %collective-permute-done.7), channel_id=1, source_target_pairs={{0,1},{1,2},{2,3},{3,4},{4,5},{5,6},{6,7},{7,8},{8,9},{9,10},{10,1... | collective-permute-start | bytes 196616 | tf_op jit(solution)/shard_map/ppermute | solution.py:120
  306.9 4.9 %collective-permute-start.9 = (bf16[256,128]{0,1:T(8,128)(2,1)S(1)}, bf16[256,128]{0,1:T(8,128)(2,1)S(1)}, u32[]{:S(2)}, u32[]{:S(2)}) collective-permute-start(bf16[256,128]{0,1:T(8,128)(2,1)S(1)} %collective-permute-done.8), channel_id=1, source_target_pairs={{0,1},{1,2},{2,3},{3,4},{4,5},{5,6},{6,7},{7,8},{8,9},{9,10},{10,1... | collective-permute-start | bytes 196616 | tf_op jit(solution)/shard_map/ppermute | solution.py:120
  311.8 4.9 %collective-permute-start.10 = (bf16[256,128]{0,1:T(8,128)(2,1)S(1)}, bf16[256,128]{0,1:T(8,128)(2,1)S(1)}, u32[]{:S(2)}, u32[]{:S(2)}) collective-permute-start(bf16[256,128]{0,1:T(8,128)(2,1)S(1)} %collective-permute-done.9), channel_id=1, source_target_pairs={{0,1},{1,2},{2,3},{3,4},{4,5},{5,6},{6,7},{7,8},{8,9},{9,10},{10,1... | collective-permute-start | bytes 196616 | tf_op jit(solution)/shard_map/ppermute | solution.py:120
  316.7 4.9 %collective-permute-start.11 = (bf16[256,128]{0,1:T(8,128)(2,1)S(1)}, bf16[256,128]{0,1:T(8,128)(2,1)S(1)}, u32[]{:S(2)}, u32[]{:S(2)}) collective-permute-start(bf16[256,128]{0,1:T(8,128)(2,1)S(1)} %collective-permute-done.10), channel_id=1, source_target_pairs={{0,1},{1,2},{2,3},{3,4},{4,5},{5,6},{6,7},{7,8},{8,9},{9,10},{10,1... | collective-permute-start | bytes 196616 | tf_op jit(solution)/shard_map/ppermute | solution.py:120
  321.6 4.9 %collective-permute-start.12 = (bf16[256,128]{0,1:T(8,128)(2,1)S(1)}, bf16[256,128]{0,1:T(8,128)(2,1)S(1)}, u32[]{:S(2)}, u32[]{:S(2)}) collective-permute-start(bf16[256,128]{0,1:T(8,128)(2,1)S(1)} %collective-permute-done.11), channel_id=1, source_target_pairs={{0,1},{1,2},{2,3},{3,4},{4,5},{5,6},{6,7},{7,8},{8,9},{9,10},{10,1... | collective-permute-start | bytes 196616 | tf_op jit(solution)/shard_map/ppermute | solution.py:120
  326.5 4.9 %collective-permute-start.13 = (bf16[256,128]{0,1:T(8,128)(2,1)S(1)}, bf16[256,128]{0,1:T(8,128)(2,1)S(1)}, u32[]{:S(2)}, u32[]{:S(2)}) collective-permute-start(bf16[256,128]{0,1:T(8,128)(2,1)S(1)} %collective-permute-done.12), channel_id=1, source_target_pairs={{0,1},{1,2},{2,3},{3,4},{4,5},{5,6},{6,7},{7,8},{8,9},{9,10},{10,1... | collective-permute-start | bytes 196616 | tf_op jit(solution)/shard_map/ppermute | solution.py:120
  331.4 4.9 %collective-permute-start.14 = (bf16[256,128]{0,1:T(8,128)(2,1)S(1)}, bf16[256,128]{0,1:T(8,128)(2,1)S(1)}, u32[]{:S(2)}, u32[]{:S(2)}) collective-permute-start(bf16[256,128]{0,1:T(8,128)(2,1)S(1)} %collective-permute-done.13), channel_id=1, source_target_pairs={{0,1},{1,2},{2,3},{3,4},{4,5},{5,6},{6,7},{7,8},{8,9},{9,10},{10,1... | collective-permute-start | bytes 196616 | tf_op jit(solution)/shard_map/ppermute | solution.py:120
  336.3 4.9 %collective-permute-start.15 = (bf16[256,128]{0,1:T(8,128)(2,1)S(1)}, bf16[256,128]{0,1:T(8,128)(2,1)S(1)}, u32[]{:S(2)}, u32[]{:S(2)}) collective-permute-start(bf16[256,128]{0,1:T(8,128)(2,1)S(1)} %collective-permute-done.14), channel_id=1, source_target_pairs={{0,1},{1,2},{2,3},{3,4},{4,5},{5,6},{6,7},{7,8},{8,9},{9,10},{10,1... | collective-permute-start | bytes 196616 | tf_op jit(solution)/shard_map/ppermute | solution.py:120
Sparse Core Ops, SparseCore 0:
  93.2 77.8 all-gather.10
  174.3 85.6 all-gather.6
  263.1 84.6 all-gather.8
